TPU v7x, 32 devices: a whole 2x2x4 slice. The times are simulated.
32 devices in a mesh: range: 4 (over y, core), chan: 8 (over z, x).
Axes of the slice: x: 2, y: 2, z: 4, core: 2. Of those that a mesh axis runs over, the one named last changes fastest.
Arguments:
- echoes: float32 [2, 64, 512, 1024], P(None, 'chan', None, 'range'), may hold values from -18 to 18
- chirp: float32 [2, 129], replicated, may hold values from -0.375 to 0.375
- train_mask: int32 [512, 8], P('chan', 'range'), may hold values from 0 to 1, as said below
Outputs:
- spectra: bfloat16 [2, 512, 64, 1024], P(None, 'chan', None, 'range')
- factors: float32 [512, 2, 128, 128], P('chan')
Inputs may be any that keep to these rules, and one draw needn't show every extreme that they name: `train_mask`: in each Doppler bin exactly 4 consecutive tiles are 0 and all other tiles are 1.
All inputs are finite; a program needn't handle non-finite values.
Results may differ from a plain program's by a relative error of at most 0.001.
Values sent between devices are 32-bit elements; how exact they have to be, the bound alone decides.
A program may use at most 128 MiB of HBM per device.

v0:
```python
import math
import jax
import jax.numpy as jnp
from jax import lax
from jax.sharding import PartitionSpec as P

TILE = 128
best_precision = lax.Precision.HIGHEST


def from_behind(value, axis, steps):
    count = lax.axis_size(axis)
    leading, last = (max(0, -steps), min(count, count - steps))
    return lax.ppermute(value, axis, [(source, source + steps) for source in range(leading, last)])


def from_behind_2(block, axis, distance):
    devices = range(lax.axis_size(axis))
    route = [((i - distance) % len(devices), i) for i in devices]
    return lax.ppermute(block, axis, route)


def toeplitz_rows(taps):
    tap_span = taps.shape[-1] - 1
    padded = jnp.concatenate([taps, jnp.zeros((taps.shape[0], tap_span), taps.dtype)], -1)
    tiled = jnp.tile(padded, (1, tap_span))
    return tiled[:, : 2 * tap_span * tap_span].reshape(taps.shape[0], tap_span, 2 * tap_span)


def compress(extended, taps):
    tap_span = taps.shape[-1] - 1
    lead_shape = extended.shape[:-1]
    block_count = extended.shape[-1] // tap_span - 1
    blocks = extended.reshape(lead_shape + (block_count + 1, tap_span))
    window = jnp.concatenate([blocks[..., :block_count, :], blocks[..., 1:, :]], -1)
    kernel = toeplitz_rows(taps)
    products = jnp.einsum(
        "tcpnk,sok->tscpno",
        window,
        kernel,
        precision=best_precision,
        preferred_element_type=jnp.float32,
    )
    real_part = products[0, 0] + products[1, 1]
    imag_part = products[1, 0] - products[0, 1]
    return jnp.stack([real_part, imag_part]).reshape(lead_shape + (block_count * tap_span,))


def doppler_table(bin_numbers, pulse_count):
    phase_index = (
        bin_numbers[:, None] * jnp.arange(pulse_count, dtype=jnp.int32)[None, :] % pulse_count
    )
    angles = phase_index.astype(jnp.float32) * (2.0 * math.pi / pulse_count)
    scaling = 1.0 / math.sqrt(pulse_count)
    return jnp.stack([jnp.cos(angles) * scaling, -jnp.sin(angles) * scaling])


def doppler(signal, dft_table):
    products = jnp.einsum(
        "sdp,tcpg->stdcg",
        dft_table,
        signal,
        precision=best_precision,
        preferred_element_type=jnp.float32,
    )
    return jnp.stack([products[0, 0] - products[1, 1], products[0, 1] + products[1, 0]])


def gram_block(spectra_now, spectra_next, weights, scaling):
    snapshot = jnp.concatenate([spectra_now, spectra_next], 2)
    masked = snapshot * weights[None, :, None, :]
    products = jnp.einsum(
        "tbkg,sblg->btskl",
        masked,
        snapshot,
        precision=best_precision,
        preferred_element_type=jnp.float32,
    )
    real_part = products[:, 0, 0] + products[:, 1, 1]
    imag_part = products[:, 0, 1] - products[:, 1, 0]
    return jnp.stack([real_part, imag_part], 1) * scaling


def factor(gram):
    order_size = gram.shape[-1]
    strip_size = min(16, order_size)
    columns = jnp.arange(order_size, dtype=jnp.int32)
    remaining = gram
    pieces = []
    for offset in range(0, order_size, strip_size):
        strip_rows = remaining[:, :, :strip_size, :]

        def column_step(position, carry):
            strip_now, found_rows = carry
            place = offset + position
            row_now = lax.dynamic_index_in_dim(strip_now, position, 2, keepdims=False)
            pivots = jnp.sum(jnp.where(columns == place, row_now[:, 0], 0.0), -1)
            inverse = lax.rsqrt(pivots)[:, None]
            row_real = jnp.where(columns >= place, row_now[:, 0] * inverse, 0.0)
            row_imag = jnp.where(columns > place, row_now[:, 1] * inverse, 0.0)
            coef_real = row_real[:, offset : offset + strip_size]
            coef_imag = row_imag[:, offset : offset + strip_size]
            new_real = (
                strip_now[:, 0]
                - coef_real[:, :, None] * row_real[:, None, :]
                - coef_imag[:, :, None] * row_imag[:, None, :]
            )
            new_imag = (
                strip_now[:, 1]
                - coef_real[:, :, None] * row_imag[:, None, :]
                + coef_imag[:, :, None] * row_real[:, None, :]
            )
            found_rows = lax.dynamic_update_index_in_dim(
                found_rows, jnp.stack([row_real, row_imag], 1), position, 2
            )
            return (jnp.stack([new_real, new_imag], 1), found_rows)

        strip_end, found_rows = lax.fori_loop(
            0, strip_size, column_step, (strip_rows, jnp.zeros_like(strip_rows))
        )
        pieces.append(found_rows)
        if offset + strip_size < order_size:
            tail_part = found_rows[:, :, :, offset + strip_size :]
            products = jnp.einsum(
                "nabi,ncbj->nacij",
                tail_part,
                found_rows,
                precision=best_precision,
                preferred_element_type=jnp.float32,
            )
            update_real = products[:, 0, 0] + products[:, 1, 1]
            update_imag = products[:, 0, 1] - products[:, 1, 0]
            remaining = remaining[:, :, strip_size:, :] - jnp.stack([update_real, update_imag], 1)
    return jnp.concatenate(pieces, 2)


def on_device(echoes, chirp, train_mask):
    tap_span = chirp.shape[-1] - 1
    pulses = echoes.shape[2]
    gate_count = echoes.shape[3]
    rim_gates = from_behind(echoes[..., :tap_span], "range", -1)
    compressed = compress(jnp.concatenate([echoes, rim_gates], -1), chirp)
    spectra_all = doppler(compressed, doppler_table(jnp.arange(pulses, dtype=jnp.int32), pulses))
    turned = lax.all_to_all(spectra_all, "chan", split_axis=1, concat_axis=2, tiled=True)
    edge_bin = from_behind_2(turned[:, :1], "chan", -1)
    following = jnp.concatenate([turned[:, 1:], edge_bin], 1)
    spectra_out = turned.astype(jnp.bfloat16)
    total_gates = gate_count * lax.axis_size("range")
    scaling = 1.0 / total_gates
    weights = jnp.broadcast_to(
        train_mask.astype(jnp.float32)[:, :, None], train_mask.shape + (TILE,)
    ).reshape(train_mask.shape[0], gate_count)
    partial_gram = lax.psum_scatter(
        gram_block(turned, following, weights, scaling), "range", scatter_dimension=0, tiled=True
    )
    factors = lax.all_gather(factor(partial_gram), "range", axis=0, tiled=True)
    return (spectra_out, factors)


def solution(mesh):
    return jax.shard_map(
        on_device,
        mesh=mesh,
        in_specs=(P(None, "chan", None, "range"), P(), P("chan", "range")),
        out_specs=(P(None, "chan", None, "range"), P("chan", None, None, None)),
        check_vma=False,
    )
```

profile of v0, /device:TPU:0, one launch (start us, length us, event | category | flops | bytes accessed | tf_op | source)
XLA Modules:
  0.0 662.5 jit_solution(18391180482651036311)
XLA Ops:
  7.2 8.7 %copy.189 = f32[2,8,512,256]{2,3,1,0:T(8,128)} copy(f32[2,8,512,256]{3,2,1,0:T(8,128)} %param.19) | data formatting | bytes 16777216 | tf_op args[0]
  30.1 6.2 pad_maximum_fusion.8
  36.3 7.0 %fusion.104 = (f32[2,8,512,2,128]{2,4,3,1,0:T(8,128)}, f32[2,8,512,2,128]{2,4,3,1,0:T(8,128)}) fusion(f32[2,8,512,3,128]{2,4,3,1,0:T(8,128)S(1)} %bitcast.399), kind=kLoop, calls=%fused_computation.288 | loop fusion | bytes 33554432 | tf_op jit(solution)/shard_map/slice | solution.py:35
  43.3 8.7 %copy.286 = f32[2,8,512,2,128]{4,2,3,1,0:T(8,128)} copy(f32[2,8,512,2,128]{2,4,3,1,0:T(8,128)} %get-tuple-element.1093) | data formatting | bytes 16777216
  52.0 8.7 %copy.285 = f32[2,8,512,2,128]{4,2,3,1,0:T(8,128)} copy(f32[2,8,512,2,128]{2,4,3,1,0:T(8,128)} %get-tuple-element.1092) | data formatting | bytes 16777216
  60.7 21.7 %fusion.55 = f32[2,2,8,512,2,128]{3,5,4,2,0,1:T(8,128)} fusion(f32[2,8,512,2,128]{4,2,3,1,0:T(8,128)} %copy.286, f32[2,8,512,2,128]{4,2,3,1,0:T(8,128)} %copy.285, f32[1,2,128,256]{3,1,2,0:T(2,128)S(1)} %bitcast.450), kind=kOutput, calls=%fused_computation.179 | convolution fusion | flops 12889096192 | bytes 33816576 | tf_op jit(solution)/shard_map/tcpnk,sok->tscpno/dot_general | solution.py:37
  82.5 10.2 %slice_add_fusion.1 = (f32[1,1,8,512,2,128]{3,5,4,2,0,1:T(8,128)S(1)}, f32[1,1,8,512,2,128]{3,5,4,2,0,1:T(8,128)}) fusion(f32[2,2,8,512,2,128]{3,5,4,2,0,1:T(8,128)} %fusion.55), kind=kLoop, calls=%fused_computation.194 | loop fusion | flops 2097152 | bytes 25165824 | tf_op jit(solution)/shard_map/add | solution.py:44
  92.6 31.7 %fusion.56 = f32[2,2,512,8,256]{2,4,0,3,1:T(8,128)S(1)} fusion(f32[1,8,512,256]{2,3,1,0:T(8,128)} %bitcast.409, f32[1,8,512,256]{2,3,1,0:T(8,128)S(1)} %bitcast.408, f32[1,512,512]{2,1,0:T(8,128)S(1)} %get-tuple-element.1118, f32[1,512,512]{2,1,0:T(8,128)S(1)} %get-tuple-element.1119), kind=kOutput, calls=%fused_computation.180 | convolution fusion | flops 25772425216 | bytes 27262976 | tf_op jit(solution)/shard_map/sdp,tcpg->stdcg/dot_general | solution.py:59
  130.7 10.3 %copy.194 = f32[2,512,8,256]{3,2,0,1:T(8,128)} copy(f32[2,512,8,256]{1,3,2,0:T(8,128)} %pad_maximum_fusion.9) | data formatting | bytes 16777216 | tf_op jit(solution)/shard_map/stack | solution.py:66
  141.1 177.9 %all_to_all.18 = f32[2,512,8,256]{3,2,0,1:T(8,128)S(1)} all-to-all(f32[2,512,8,256]{3,2,0,1:T(8,128)} %copy.194), channel_id=1, replica_groups=mesh['range'=4,'chan'=8] {'chan'}, dimensions={1} | all-to-all | bytes 16777216 | tf_op jit(solution)/shard_map/all_to_all | solution.py:144
  329.2 7.6 %slice.768 = f32[2,63,64,256]{3,2,0,1:T(8,128)} slice(f32[2,64,64,256]{3,2,0,1:T(8,128)} %bitcast.402), slice={[0:2], [1:64], [0:64], [0:256]} | slice | bytes 16515072 | tf_op jit(solution)/shard_map/slice | solution.py:146
  336.8 27.5 %fusion.46 = f32[64,2,2,128,128]{3,4,1,2,0:T(8,128)} fusion(f32[2,1,64,256]{3,2,0,1:T(8,128)S(1)} %collective-permute-done.1, f32[2,63,64,256]{3,2,0,1:T(8,128)} %slice.768, f32[2,64,64,256]{3,2,0,1:T(8,128)} %bitcast.403, f32[64,256]{1,0:T(8,128)S(1)} %bitcast.452), kind=kOutput, calls=%fused_computation.169 | convolution fusion | flops 12905873408 | bytes 33619968 | tf_op jit(solution)/shard_map/tbkg,sblg->btskl/dot_general | solution.py:72
  375.5 8.0 %copy.365 = f32[8,8,256,128]{3,1,2,0:T(8,128)} copy(f32[8,8,256,128]{3,2,1,0:T(8,128)S(1)} %bitcast.404) | data formatting | bytes 16777216
  383.6 82.1 %reduce-scatter.5.cloned.1.call-done = f32[16,32768]{1,0:T(8,128)} async-done(((f32[64,32768]{1,0:T(8,128)}), f32[16,32768]{1,0:T(8,128)}) %reduce-scatter.5.cloned.1.call-update) | async-done | bytes 2097168
  470.2 8.8 %while.136 = (s32[]{:T(128)}, f32[16,2,16,128]{3,2,1,0:T(8,128)S(1)}, f32[16,2,16,128]{3,0,1,2:T(8,128)S(1)}, s32[]{:T(128)}) while((s32[]{:T(128)}, f32[16,2,16,128]{3,2,1,0:T(8,128)S(1)}, f32[16,2,16,128]{3,0,1,2:T(8,128)S(1)}, s32[]{:T(128)}) %tuple.404), condition=%wide.region_3.4_spmd.clone.clone, body=%wide.region_1.3_spmd.clone.clone.sunk | while | flops 345458 | bytes 1227949 | solution.py:118
  488.1 11.2 %while.137 = (s32[]{:T(128)}, f32[16,2,16,128]{3,2,1,0:T(8,128)S(1)}, f32[16,2,16,128]{3,0,1,2:T(8,128)S(1)}, s32[]{:T(128)}, s32[]{:T(128)}) while((s32[]{:T(128)}, f32[16,2,16,128]{3,2,1,0:T(8,128)S(1)}, f32[16,2,16,128]{3,0,1,2:T(8,128)S(1)}, s32[]{:T(128)}, s32[]{:T(128)}) %tuple.407), condition=%wide.region_6.7_spmd.clone.clone, body=%wide.region_4.6_spmd.clone.clone.sunk | while | flops 345459 | bytes 1228033 | solution.py:118
  504.7 11.2 %while.138 = (s32[]{:T(128)}, f32[16,2,16,128]{3,2,1,0:T(8,128)S(1)}, f32[16,2,16,128]{3,0,1,2:T(8,128)S(1)}, s32[]{:T(128)}, s32[]{:T(128)}) while((s32[]{:T(128)}, f32[16,2,16,128]{3,2,1,0:T(8,128)S(1)}, f32[16,2,16,128]{3,0,1,2:T(8,128)S(1)}, s32[]{:T(128)}, s32[]{:T(128)}) %tuple.410), condition=%wide.region_9.10_spmd.clone.clone, body=%wide.region_7.9_spmd.clone.clone.sunk | while | flops 345459 | bytes 1228033 | solution.py:118
  519.6 11.4 %while.139 = (s32[]{:T(128)}, f32[16,2,16,128]{3,2,1,0:T(8,128)S(1)}, f32[16,2,16,128]{3,0,1,2:T(8,128)S(1)}, s32[]{:T(128)}, s32[]{:T(128)}) while((s32[]{:T(128)}, f32[16,2,16,128]{3,2,1,0:T(8,128)S(1)}, f32[16,2,16,128]{3,0,1,2:T(8,128)S(1)}, s32[]{:T(128)}, s32[]{:T(128)}) %tuple.413), condition=%wide.region_12.13_spmd.clone.clone, body=%wide.region_10.12_spmd.clone.clone.sunk | while | flops 345459 | bytes 1228033 | solution.py:118
  534.4 11.2 %while.140 = (s32[]{:T(128)}, f32[16,2,16,128]{3,2,1,0:T(8,128)S(1)}, f32[16,2,16,128]{3,0,1,2:T(8,128)S(1)}, s32[]{:T(128)}, s32[]{:T(128)}) while((s32[]{:T(128)}, f32[16,2,16,128]{3,2,1,0:T(8,128)S(1)}, f32[16,2,16,128]{3,0,1,2:T(8,128)S(1)}, s32[]{:T(128)}, s32[]{:T(128)}) %tuple.416), condition=%wide.region_15.16_spmd.clone.clone, body=%wide.region_13.15_spmd.clone.clone.sunk | while | flops 345459 | bytes 1228033 | solution.py:118
  548.3 11.2 %while.141 = (s32[]{:T(128)}, f32[16,2,16,128]{3,2,1,0:T(8,128)S(1)}, f32[16,2,16,128]{3,0,1,2:T(8,128)S(1)}, s32[]{:T(128)}, s32[]{:T(128)}) while((s32[]{:T(128)}, f32[16,2,16,128]{3,2,1,0:T(8,128)S(1)}, f32[16,2,16,128]{3,0,1,2:T(8,128)S(1)}, s32[]{:T(128)}, s32[]{:T(128)}) %tuple.419), condition=%wide.region_18.19_spmd.clone.clone, body=%wide.region_16.18_spmd.clone.clone.sunk | while | flops 345459 | bytes 1228033 | solution.py:118
  561.9 11.2 %while.142 = (s32[]{:T(128)}, f32[16,2,16,128]{3,2,1,0:T(8,128)S(1)}, f32[16,2,16,128]{3,0,1,2:T(8,128)S(1)}, s32[]{:T(128)}, s32[]{:T(128)}) while((s32[]{:T(128)}, f32[16,2,16,128]{3,2,1,0:T(8,128)S(1)}, f32[16,2,16,128]{3,0,1,2:T(8,128)S(1)}, s32[]{:T(128)}, s32[]{:T(128)}) %tuple.422), condition=%wide.region_21.22_spmd.clone.clone, body=%wide.region_19.21_spmd.clone.clone.sunk | while | flops 345459 | bytes 1228033 | solution.py:118
  575.4 13.0 %while.143 = (s32[]{:T(128)}, f32[16,2,16,128]{3,2,1,0:T(8,128)S(1)}, f32[16,2,16,128]{3,2,1,0:T(8,128)S(1)}, s32[]{:T(128)}, s32[]{:T(128)}, /*index=5*/s32[]{:T(128)}) while((s32[]{:T(128)}, f32[16,2,16,128]{3,2,1,0:T(8,128)S(1)}, f32[16,2,16,128]{3,2,1,0:T(8,128)S(1)}, s32[]{:T(128)}, s32[]{:T(128)}, ...), condition=%wide.region_24.25_spmd.clone.clone, body=%wide.region_22.24_spmd.clone.clone.sunk | while | flops 345459 | bytes 1293577 | solution.py:118
  595.5 52.1 %all-gather.2.cloned.1.call-done = f32[64,2,128,128]{3,2,1,0:T(8,128)} async-done(((f32[16,2,128,128]{3,2,1,0:T(8,128)}), f32[64,2,128,128]{3,2,1,0:T(8,128)}) %all-gather.2.cloned.1.call-update) | async-done | bytes 8388624 | tf_op jit(solution)/shard_map/all_gather | solution.py:156
  647.6 7.9 %copy.476 = f32[64,2,128,128]{3,2,1,0:T(8,128)} copy(f32[64,2,128,128]{3,2,1,0:T(8,128)} %all-gather.2.cloned.1.call-done) | data formatting | bytes 16777216
  (1766 shorter events, 161.7 us)
Async XLA Ops:
  7.2 458.5 %reduce-scatter.5.cloned.1.call-start = ((), (), s32[]{:S(2)}) async-start(), calls=%async_computation.3 | async-start | bytes 10485760
  15.9 6.1 copy-start.6
  20.7 9.4 %collective-permute-start = (f32[2,8,512,128]{2,3,1,0:T(8,128)}, f32[2,8,512,128]{2,3,1,0:T(8,128)}, u32[]{:S(2)}, u32[]{:S(2)}) collective-permute-start(f32[2,8,512,128]{2,3,1,0:T(8,128)} %slice.757), channel_id=1, source_target_pairs={{8,0},{16,8},{24,16},{9,1},{17,9},{25,17},{10,2},{18,10},{26,18},{... | collective-permute-start | bytes 12582920 | tf_op jit(solution)/shard_map/ppermute | solution.py:14
  22.6 13.7 %copy-start.5 = (f32[2,32896]{1,0:T(2,128)}, f32[2,32896]{1,0:T(2,128)S(1)}, u32[]{:S(2)}) copy-start(f32[2,32896]{1,0:T(2,128)S(1)} %tile.10) | copy-start | bytes 789508
  52.0 8.7 %slice-start = ((f32[2,32896]{1,0:T(2,128)}), f32[2,32768]{1,0:T(2,128)S(1)}, s32[]{:S(2)}) async-start(f32[2,32896]{1,0:T(2,128)} %copy-done.5), calls=%async_computation.4 | async-start | bytes 524288 | tf_op jit(solution)/shard_map/slice | solution.py:27
  319.0 3.5 copy-start
  319.0 9.9 %copy-start.7 = (s32[64,2]{0,1:T(2,128)S(1)}, s32[64,2]{0,1:T(2,128)}, u32[]{:S(2)}) copy-start(s32[64,2]{0,1:T(2,128)} %param.21) | copy-start | bytes 1540
  322.5 3.3 copy-start.1
  325.8 11.0 %collective-permute-start.1 = (f32[2,1,64,256]{3,2,0,1:T(8,128)S(1)}, f32[2,1,64,256]{3,2,0,1:T(8,128)S(1)}, u32[]{:S(2)}, u32[]{:S(2)}) collective-permute-start(f32[2,1,64,256]{3,2,0,1:T(8,128)S(1)} %slice.769), channel_id=1, source_target_pairs={{1,0},{2,1},{3,2},{4,3},{5,4},{6,5},{7,6},{0,7},{9,8},{10,9},{11,1... | collective-permute-start | bytes 393224 | tf_op jit(solution)/shard_map/ppermute | solution.py:20
  383.6 264.0 %all-gather.2.cloned.1.call-start = ((), (), s32[]{:S(2)}) async-start(), calls=%async_computation.2 | async-start | bytes 10485760 | tf_op jit(solution)/shard_map/all_gather | solution.py:156
  479.9 4.4 copy-start.2
  503.5 1.1 copy-start.3
  515.9 3.5 copy-start.4
Sparse Core Ops, SparseCore 0:
  383.7 81.9 reduce-scatter.4
  589.3 58.2 all-gather.1
where the time goes:
time: 668 us; the launch traced here: 663 us
  blocking collectives  178 us (27%)
  waiting for transfers between devices  138 us (21%)
  local copies, waits for them, and re-layouts  124 us (19%)
  other arithmetic  98.7 us (15%)
  matrix products  95.1 us (14%)
  between operations  14.8 us (2%)
  loops' own time  9.7 us (1%)
    all_to_all x1, blocking collectives, on_device(): lax.all_to_all(spectra_all, 'chan', split_axis=1, concat_axis=2, tiled=True)  178 us
    unnamed x3, waiting for transfers between devices  82.1 us
    unnamed x35, local copies, waits for them, and re-layouts  57.4 us
    all_gather x1, waiting for transfers between devices, on_device(): factors = lax.all_gather(factor(partial_gram), 'range', axis=0, tiled=True)  52.1 us
    dot_general x1, matrix products, doppler(): jnp.einsum('sdp,tcpg->stdcg', dft_table, signal, precision=best_precision...  31.7 us
    dot_general x1, matrix products, gram_block(): jnp.einsum('tbkg,sblg->btskl', masked, snapshot, precision=best_precision...  27.5 us
    dot_general x1, matrix products, compress(): jnp.einsum('tcpnk,sok->tscpno', window, kernel, precision=best_precision,...  21.7 us
    select_n x256, other arithmetic, column_step(): row_real = jnp.where(columns >= place, row_now[:, 0] * inverse, 0.0)  19 us
  transfers between devices with their start and end apart: 4, of which 3 were waited for; matrix products, arithmetic and copies ran while one was open for 3% of the time, Pallas kernels for 0%

commit v1 on v0

--- a/solution.py
+++ b/solution.py
@@ -141,7 +141,9 @@
     rim_gates = from_behind(echoes[..., :tap_span], "range", -1)
     compressed = compress(jnp.concatenate([echoes, rim_gates], -1), chirp)
     spectra_all = doppler(compressed, doppler_table(jnp.arange(pulses, dtype=jnp.int32), pulses))
-    turned = lax.all_to_all(spectra_all, "chan", split_axis=1, concat_axis=2, tiled=True)
+    parts = jnp.split(spectra_all, lax.axis_size("chan"), axis=1)
+    received = lax.all_to_all(jnp.stack(parts), "chan", 0, 0)
+    turned = jnp.concatenate(received, axis=2)
     edge_bin = from_behind_2(turned[:, :1], "chan", -1)
     following = jnp.concatenate([turned[:, 1:], edge_bin], 1)
     spectra_out = turned.astype(jnp.bfloat16)

time: 668 us -> 680 us (1.018)
  other arithmetic: 98.7 us -> 108 us
    unnamed x0 -> x7, other arithmetic: none -> 12.4 us
    unnamed x35 -> x34, local copies, waits for them, and re-layouts: 57.4 us -> 59.9 us
where the time goes in v1:
time: 680 us; the launch traced here: 675 us
  blocking collectives  178 us (26%)
  waiting for transfers between devices  138 us (20%)
  local copies, waits for them, and re-layouts  128 us (19%)
  other arithmetic  108 us (16%)
  matrix products  93.8 us (14%)
  between operations  15.1 us (2%)
  loops' own time  9.84 us (1%)
    all_to_all x1, blocking collectives, on_device(): received = lax.all_to_all(jnp.stack(parts), 'chan', 0, 0)  178 us
    unnamed x3, waiting for transfers between devices  82.1 us
    unnamed x34, local copies, waits for them, and re-layouts  59.9 us
    all_gather x1, waiting for transfers between devices, on_device(): factors = lax.all_gather(factor(partial_gram), 'range', axis=0, tiled=True)  52.4 us
    dot_general x1, matrix products, doppler(): jnp.einsum('sdp,tcpg->stdcg', dft_table, signal, precision=best_precision...  31.9 us
    dot_general x1, matrix products, gram_block(): jnp.einsum('tbkg,sblg->btskl', masked, snapshot, precision=best_precision...  26 us
    dot_general x1, matrix products, compress(): jnp.einsum('tcpnk,sok->tscpno', window, kernel, precision=best_precision,...  21.7 us
    select_n x256, other arithmetic, column_step(): row_real = jnp.where(columns >= place, row_now[:, 0] * inverse, 0.0)  19 us
  transfers between devices with their start and end apart: 4, of which 3 were waited for; matrix products, arithmetic and copies ran while one was open for 3% of the time, Pallas kernels for 0%

profile of v1, /device:TPU:0, one launch (start us, length us, event | category | flops | bytes accessed | tf_op | source)
XLA Modules:
  0.0 674.7 jit_solution(15937365246078017848)
XLA Ops:
  7.2 8.7 %copy.190 = f32[2,8,512,256]{2,3,1,0:T(8,128)} copy(f32[2,8,512,256]{3,2,1,0:T(8,128)} %param.19) | data formatting | bytes 16777216 | tf_op args[0]
  30.1 6.2 pad_maximum_fusion.8
  36.3 7.0 %fusion.127 = (f32[2,8,512,2,128]{2,4,3,1,0:T(8,128)}, f32[2,8,512,2,128]{2,4,3,1,0:T(8,128)}) fusion(f32[2,8,512,3,128]{2,4,3,1,0:T(8,128)S(1)} %bitcast.433), kind=kLoop, calls=%fused_computation.325 | loop fusion | bytes 33554432 | tf_op jit(solution)/shard_map/slice | solution.py:35
  43.3 8.7 %copy.286 = f32[2,8,512,2,128]{4,2,3,1,0:T(8,128)} copy(f32[2,8,512,2,128]{2,4,3,1,0:T(8,128)} %get-tuple-element.1086) | data formatting | bytes 16777216
  52.0 8.7 %copy.287 = f32[2,8,512,2,128]{4,2,3,1,0:T(8,128)} copy(f32[2,8,512,2,128]{2,4,3,1,0:T(8,128)} %get-tuple-element.1087) | data formatting | bytes 16777216
  60.7 21.7 %fusion.55 = f32[2,2,8,512,2,128]{3,5,4,2,0,1:T(8,128)} fusion(f32[2,8,512,2,128]{4,2,3,1,0:T(8,128)} %copy.287, f32[2,8,512,2,128]{4,2,3,1,0:T(8,128)} %copy.286, f32[1,2,128,256]{3,1,2,0:T(2,128)S(1)} %bitcast.483), kind=kOutput, calls=%fused_computation.192 | convolution fusion | flops 12889096192 | bytes 33816576 | tf_op jit(solution)/shard_map/tcpnk,sok->tscpno/dot_general | solution.py:37
  82.4 10.2 %slice_add_fusion.1 = (f32[1,1,8,512,2,128]{3,5,4,2,0,1:T(8,128)S(1)}, f32[1,1,8,512,2,128]{3,5,4,2,0,1:T(8,128)}) fusion(f32[2,2,8,512,2,128]{3,5,4,2,0,1:T(8,128)} %fusion.55), kind=kLoop, calls=%fused_computation.207 | loop fusion | flops 2097152 | bytes 25165824 | tf_op jit(solution)/shard_map/add | solution.py:44
  92.6 31.9 %fusion.56 = f32[2,2,512,8,256]{2,4,0,3,1:T(8,128)S(1)} fusion(f32[1,8,512,256]{2,3,1,0:T(8,128)} %bitcast.441, f32[1,8,512,256]{2,3,1,0:T(8,128)S(1)} %bitcast.440, f32[1,512,512]{2,1,0:T(8,128)S(1)} %get-tuple-element.1112, f32[1,512,512]{2,1,0:T(8,128)S(1)} %get-tuple-element.1113), kind=kOutput, calls=%fused_computation.193 | convolution fusion | flops 25772425216 | bytes 27262976 | tf_op jit(solution)/shard_map/sdp,tcpg->stdcg/dot_general | solution.py:59
  140.9 12.8 %copy.195 = f32[8,2,64,8,256]{4,3,2,1,0:T(8,128)} copy(f32[8,2,64,8,256]{2,4,3,1,0:T(8,128)} %fusion.85) | data formatting | bytes 16777216 | tf_op jit(solution)/shard_map/stack | solution.py:145
  153.7 177.9 %all_to_all.5 = f32[8,2,64,8,256]{4,3,2,1,0:T(8,128)S(1)} all-to-all(f32[8,2,64,8,256]{4,3,2,1,0:T(8,128)} %copy.195), channel_id=1, replica_groups=mesh['range'=4,'chan'=8] {'chan'}, dimensions={0} | all-to-all | bytes 16777216 | tf_op jit(solution)/shard_map/all_to_all | solution.py:145
  349.5 26.0 %fusion.46 = f32[64,2,2,128,128]{3,4,1,2,0:T(8,128)} fusion(f32[2,1,64,256]{3,2,0,1:T(8,128)S(1)} %collective-permute-done.1, f32[2,63,64,256]{3,2,0,1:T(8,128)} %copy.381, f32[64,256]{1,0:T(8,128)S(1)} %bitcast.485, f32[8,2,64,8,256]{4,3,2,1,0:T(8,128)} %copy-done), kind=kOutput, calls=%fused_computation.183 | convolution fusion | flops 12905873408 | bytes 33619968 | tf_op jit(solution)/shard_map/tbkg,sblg->btskl/dot_general | solution.py:72
  386.8 8.0 %copy.376 = f32[8,8,256,128]{3,1,2,0:T(8,128)} copy(f32[8,8,256,128]{3,2,1,0:T(8,128)S(1)} %bitcast.437) | data formatting | bytes 16777216
  394.9 82.0 %reduce-scatter.5.cloned.1.call-done = f32[16,32768]{1,0:T(8,128)} async-done(((f32[64,32768]{1,0:T(8,128)}), f32[16,32768]{1,0:T(8,128)}) %reduce-scatter.5.cloned.1.call-update) | async-done | bytes 2097168
  479.5 8.8 %while.136 = (s32[]{:T(128)}, f32[16,2,16,128]{3,2,1,0:T(8,128)S(1)}, f32[16,2,16,128]{3,0,1,2:T(8,128)S(1)}, s32[]{:T(128)}) while((s32[]{:T(128)}, f32[16,2,16,128]{3,2,1,0:T(8,128)S(1)}, f32[16,2,16,128]{3,0,1,2:T(8,128)S(1)}, s32[]{:T(128)}) %tuple.401), condition=%wide.region_3.4_spmd.clone.clone, body=%wide.region_1.3_spmd.clone.clone.sunk | while | flops 345458 | bytes 1227941 | solution.py:118
  500.4 11.1 %while.137 = (s32[]{:T(128)}, f32[16,2,16,128]{3,2,1,0:T(8,128)S(1)}, f32[16,2,16,128]{3,0,1,2:T(8,128)S(1)}, s32[]{:T(128)}, s32[]{:T(128)}) while((s32[]{:T(128)}, f32[16,2,16,128]{3,2,1,0:T(8,128)S(1)}, f32[16,2,16,128]{3,0,1,2:T(8,128)S(1)}, s32[]{:T(128)}, s32[]{:T(128)}) %tuple.404), condition=%wide.region_6.7_spmd.clone.clone, body=%wide.region_4.6_spmd.clone.clone.sunk | while | flops 345459 | bytes 1228025 | solution.py:118
  517.0 11.1 %while.138 = (s32[]{:T(128)}, f32[16,2,16,128]{3,2,1,0:T(8,128)S(1)}, f32[16,2,16,128]{3,0,1,2:T(8,128)S(1)}, s32[]{:T(128)}, s32[]{:T(128)}) while((s32[]{:T(128)}, f32[16,2,16,128]{3,2,1,0:T(8,128)S(1)}, f32[16,2,16,128]{3,0,1,2:T(8,128)S(1)}, s32[]{:T(128)}, s32[]{:T(128)}) %tuple.407), condition=%wide.region_9.10_spmd.clone.clone, body=%wide.region_7.9_spmd.clone.clone.sunk | while | flops 345459 | bytes 1228025 | solution.py:118
  531.8 11.4 %while.139 = (s32[]{:T(128)}, f32[16,2,16,128]{3,2,1,0:T(8,128)S(1)}, f32[16,2,16,128]{3,0,1,2:T(8,128)S(1)}, s32[]{:T(128)}, s32[]{:T(128)}) while((s32[]{:T(128)}, f32[16,2,16,128]{3,2,1,0:T(8,128)S(1)}, f32[16,2,16,128]{3,0,1,2:T(8,128)S(1)}, s32[]{:T(128)}, s32[]{:T(128)}) %tuple.410), condition=%wide.region_12.13_spmd.clone.clone, body=%wide.region_10.12_spmd.clone.clone.sunk | while | flops 345459 | bytes 1228025 | solution.py:118
  546.5 11.1 %while.140 = (s32[]{:T(128)}, f32[16,2,16,128]{3,2,1,0:T(8,128)S(1)}, f32[16,2,16,128]{3,0,1,2:T(8,128)S(1)}, s32[]{:T(128)}, s32[]{:T(128)}) while((s32[]{:T(128)}, f32[16,2,16,128]{3,2,1,0:T(8,128)S(1)}, f32[16,2,16,128]{3,0,1,2:T(8,128)S(1)}, s32[]{:T(128)}, s32[]{:T(128)}) %tuple.413), condition=%wide.region_15.16_spmd.clone.clone, body=%wide.region_13.15_spmd.clone.clone.sunk | while | flops 345459 | bytes 1228025 | solution.py:118
  560.4 11.1 %while.141 = (s32[]{:T(128)}, f32[16,2,16,128]{3,2,1,0:T(8,128)S(1)}, f32[16,2,16,128]{3,0,1,2:T(8,128)S(1)}, s32[]{:T(128)}, s32[]{:T(128)}) while((s32[]{:T(128)}, f32[16,2,16,128]{3,2,1,0:T(8,128)S(1)}, f32[16,2,16,128]{3,0,1,2:T(8,128)S(1)}, s32[]{:T(128)}, s32[]{:T(128)}) %tuple.416), condition=%wide.region_18.19_spmd.clone.clone, body=%wide.region_16.18_spmd.clone.clone.sunk | while | flops 345459 | bytes 1228025 | solution.py:118
  574.0 11.1 %while.142 = (s32[]{:T(128)}, f32[16,2,16,128]{3,2,1,0:T(8,128)S(1)}, f32[16,2,16,128]{3,0,1,2:T(8,128)S(1)}, s32[]{:T(128)}, s32[]{:T(128)}) while((s32[]{:T(128)}, f32[16,2,16,128]{3,2,1,0:T(8,128)S(1)}, f32[16,2,16,128]{3,0,1,2:T(8,128)S(1)}, s32[]{:T(128)}, s32[]{:T(128)}) %tuple.419), condition=%wide.region_21.22_spmd.clone.clone, body=%wide.region_19.21_spmd.clone.clone.sunk | while | flops 345459 | bytes 1228025 | solution.py:118
  586.6 12.9 %while.143 = (s32[]{:T(128)}, f32[16,2,16,128]{3,2,1,0:T(8,128)S(1)}, f32[16,2,16,128]{3,2,1,0:T(8,128)S(1)}, s32[]{:T(128)}, s32[]{:T(128)}, /*index=5*/s32[]{:T(128)}) while((s32[]{:T(128)}, f32[16,2,16,128]{3,2,1,0:T(8,128)S(1)}, f32[16,2,16,128]{3,2,1,0:T(8,128)S(1)}, s32[]{:T(128)}, s32[]{:T(128)}, ...), condition=%wide.region_24.25_spmd.clone.clone, body=%wide.region_22.24_spmd.clone.clone.sunk | while | flops 345459 | bytes 1293569 | solution.py:118
  601.1 6.1 copy.379
  607.2 52.4 %all-gather.2.cloned.1.call-done = f32[64,2,128,128]{3,2,1,0:T(8,128)} async-done(((f32[16,2,128,128]{3,2,1,0:T(8,128)}), f32[64,2,128,128]{3,2,1,0:T(8,128)}) %all-gather.2.cloned.1.call-update) | async-done | bytes 8388624 | tf_op jit(solution)/shard_map/all_gather | solution.py:158
  659.6 7.9 %copy.496 = f32[64,2,128,128]{3,2,1,0:T(8,128)} copy(f32[64,2,128,128]{3,2,1,0:T(8,128)} %all-gather.2.cloned.1.call-done) | data formatting | bytes 16777216
  (1772 shorter events, 173.7 us)
Async XLA Ops:
  7.2 469.7 %reduce-scatter.5.cloned.1.call-start = ((), (), s32[]{:S(2)}) async-start(), calls=%async_computation.3 | async-start | bytes 10485760
  15.9 6.1 copy-start.5
  20.7 9.4 %collective-permute-start = (f32[2,8,512,128]{2,3,1,0:T(8,128)}, f32[2,8,512,128]{2,3,1,0:T(8,128)}, u32[]{:S(2)}, u32[]{:S(2)}) collective-permute-start(f32[2,8,512,128]{2,3,1,0:T(8,128)} %slice.757), channel_id=1, source_target_pairs={{8,0},{16,8},{24,16},{9,1},{17,9},{25,17},{10,2},{18,10},{26,18},{... | collective-permute-start | bytes 12582920 | tf_op jit(solution)/shard_map/ppermute | solution.py:14
  22.6 13.7 %copy-start.4 = (f32[2,32896]{1,0:T(2,128)}, f32[2,32896]{1,0:T(2,128)S(1)}, u32[]{:S(2)}) copy-start(f32[2,32896]{1,0:T(2,128)S(1)} %tile.10) | copy-start | bytes 789508
  52.0 8.7 %slice-start = ((f32[2,32896]{1,0:T(2,128)}), f32[2,32768]{1,0:T(2,128)S(1)}, s32[]{:S(2)}) async-start(f32[2,32896]{1,0:T(2,128)} %copy-done.4), calls=%async_computation.4 | async-start | bytes 524288 | tf_op jit(solution)/shard_map/slice | solution.py:27
  331.6 3.5 copy-start
  331.6 9.9 %copy-start.6 = (s32[64,2]{0,1:T(2,128)S(1)}, s32[64,2]{0,1:T(2,128)}, u32[]{:S(2)}) copy-start(s32[64,2]{0,1:T(2,128)} %param.21) | copy-start | bytes 1540
  335.1 3.3 copy-start.1
  338.4 11.1 %collective-permute-start.1 = (f32[2,1,64,256]{3,2,0,1:T(8,128)S(1)}, f32[2,1,64,256]{3,2,0,1:T(8,128)S(1)}, u32[]{:S(2)}, u32[]{:S(2)}) collective-permute-start(f32[2,1,64,256]{3,2,0,1:T(8,128)S(1)} %copy.380), channel_id=1, source_target_pairs={{1,0},{2,1},{3,2},{4,3},{5,4},{6,5},{7,6},{0,7},{9,8},{10,9},{11,1... | collective-permute-start | bytes 393224 | tf_op jit(solution)/shard_map/ppermute | solution.py:20
  394.8 264.8 %all-gather.2.cloned.1.call-start = ((), (), s32[]{:S(2)}) async-start(), calls=%async_computation.2 | async-start | bytes 10485760 | tf_op jit(solution)/shard_map/all_gather | solution.py:158
  515.7 1.1 copy-start.2
  528.1 3.5 copy-start.3
Sparse Core Ops, SparseCore 0:
  394.9 81.9 reduce-scatter.4
  601.3 58.2 all-gather.1
